TPU v7x, 32 devices: a whole 2x2x4 slice. The times are simulated.
32 devices in a mesh: mem: 8 (over z, y), lat: 4 (over x, core).
Axes of the slice: x: 2, y: 2, z: 4, core: 2. Of those that a mesh axis runs over, the one named last changes fastest.
Arguments:
- replica_variables: float32 [8, 4, 64, 4096], P('mem', None, 'lat'), may hold values from -40 to 40, as said below
- analysis: float32 [4, 64, 4096], P(None, 'lat'), may hold values from -4 to 4
- labels: int32 [64, 32], P('lat'), may hold values from 0 to 7, as said below
- pairing: int32 [8], replicated, may hold values from 0 to 7, as said below
Outputs:
- closing_ensemble_values: float32 [8, 4, 64, 4096], P('mem', None, 'lat')
- factor: float32 [8, 8], P('mem')
Inputs may be any that keep to these rules, and one draw needn't show every extreme that they name: `replica_variables`: member fields; the spread of members differs across rows and columns. `labels`: every label value occurs at least once. pairing[pairing[m]] = m and pairing[m] != m for every member m.
All inputs are finite; a program needn't handle non-finite values.
Results may differ from a plain program's by a relative error of at most 0.00015.
Values sent between devices are 32-bit elements; how exact they have to be, the bound alone decides.
A program may use at most 64 MiB of HBM per device.

v0:
```python
import functools

import jax
import jax.numpy as jnp
from jax import lax
from jax.experimental import pallas as pl
from jax.experimental.pallas import tpu as pltpu
from jax.sharding import PartitionSpec as P

MESH = pl.DeviceIdType.MESH
TILE = 128
REGIONS = 8
STEPS = 3
MAX_BRANCHES = 28
HALO = 2 * STEPS
VMEM_LIMIT = 24 * 2**20
FIELDS = 4
REACH = (2 * STEPS - 1, 2 * STEPS - 1, 2 * STEPS, STEPS)


grav_coef = 0.1
depth_coef = 0.1
advect_coef = 0.05
diffuse_coef = 0.05
coriolis_coef = 0.05
target_size = 0.5
small_eps = 1e-06


def shift_lon(plane):
    sub = plane.shape[0]
    lane = lax.broadcasted_iota(jnp.int32, plane.shape, 1)
    east = pltpu.roll(plane, TILE - 1, 1)
    east = jnp.where(lane == TILE - 1, pltpu.roll(east, sub - 1, 0), east)
    west = pltpu.roll(plane, 1, 1)
    west = jnp.where(lane == 0, pltpu.roll(west, 1, 0), west)
    return east, west


def diff_lon(plane):
    east, west = shift_lon(plane)
    return east - west


def run_steps(state, buf, spare, local_rows, sub, start, rows_all):
    extent = local_rows + 2 * HALO

    def at(field, e):
        return pl.ds((field * extent + e) * sub, sub)

    def masked(e, plane):
        if HALO <= e < HALO + local_rows:
            return plane
        row = start + (e - HALO)
        return jnp.where((row >= 0) & (row < rows_all), 1.0, 0.0).astype(jnp.float32) * plane

    def coriolis(e):
        row = (start + (e - HALO)).astype(jnp.float32)
        return coriolis_coef * (2.0 * (row + 0.5) / rows_all - 1.0)

    tracer_source, source_field = state, 3
    for step in range(STEPS):
        margin = 2 * (STEPS - 1 - step)
        narrow = STEPS - 1 - step
        target, target_field = (spare, 0) if step % 2 == 0 else (buf, 3)
        own = (HALO, HALO + local_rows)
        for e in range(own[0] - margin - 1, own[1] + margin + 1):
            divergence = diff_lon(state[at(1, e), :]) + state[at(2, e + 1), :] - state[at(2, e - 1), :]
            buf[at(0, e), :] = masked(e, state[at(0, e), :] - depth_coef * divergence)
        for e in range(own[0] - margin, own[1] + margin):
            f = coriolis(e)
            v = state[at(2, e), :]
            u1 = state[at(1, e), :] + f * v - grav_coef * diff_lon(buf[at(0, e), :])
            slope = buf[at(0, e + 1), :] - buf[at(0, e - 1), :]
            buf[at(1, e), :] = u1
            buf[at(2, e), :] = masked(e, v - f * u1 - grav_coef * slope)
        for e in range(own[0] - narrow, own[1] + narrow):
            q = tracer_source[at(source_field, e), :]
            upper = tracer_source[at(source_field, e + 1), :]
            lower = tracer_source[at(source_field, e - 1), :]
            east, west = shift_lon(q)
            advected = buf[at(1, e), :] * (east - west) + buf[at(2, e), :] * (upper - lower)
            spreading = east + west + upper + lower - 4.0 * q
            target[at(target_field, e), :] = masked(e, q - advect_coef * advected + diffuse_coef * spreading)
        state = buf
        tracer_source, source_field = target, target_field
    return [(buf, 0), (buf, 1), (buf, 2), (tracer_source, source_field)]


def pairs_of(size):
    return [(a, b) for a in range(size) for b in range(a + 1, size)]


def pair_index(pairing_ref):
    size = pairing_ref.shape[0]
    me = lax.axis_index("mem")
    partner = pairing_ref[me]
    low, high = jnp.minimum(me, partner), jnp.maximum(me, partner)
    return low * (2 * size - low - 1) // 2 + high - low - 1


def steps_kernel(size, local_rows, sub, as_rows, *refs):
    extent = local_rows + 2 * HALO
    if as_rows:
        state_ref, factor_ref, out_ref, factor_out, buf, spare = refs
        factor_out[...] = factor_ref[...]
    else:
        state_ref, pairing_ref, out_ref, index_ref, buf, spare = refs
        index_ref[0, 0] = pair_index(pairing_ref)
    lat = lax.axis_index("lat")
    fields = run_steps(state_ref, buf, spare, local_rows, sub, lat * local_rows, local_rows * size)
    for field, (ref, place) in enumerate(fields):
        if not as_rows:
            for tile in range(local_rows * sub // 8):
                column = (field * local_rows * sub // 8 + tile) * TILE
                out_ref[:, column : column + TILE] = ref[pl.ds((place * extent + HALO) * sub + tile * 8, 8), :]
            continue
        for row in range(0, local_rows, 8):
            for t in range(sub):
                first = (place * extent + HALO + row) * sub + t
                out_ref[field, row : row + 8, t * TILE : (t + 1) * TILE] = ref[pl.ds(first, 8, stride=sub), :]


def halo_copies(buf, local_rows, sub, lat, size, send_sem, recv_sem):
    extent = local_rows + 2 * HALO
    mem = lax.axis_index("mem")
    copies = []
    for side, peer in ((0, lat - 1), (1, lat + 1)):
        group = []
        for field in range(FIELDS):
            reach = REACH[field]
            source = HALO if side == 0 else HALO + local_rows - reach
            target = HALO + local_rows if side == 0 else HALO - reach
            group.append(
                pltpu.make_async_remote_copy(
                    src_ref=buf.at[pl.ds((field * extent + source) * sub, reach * sub), :],
                    dst_ref=buf.at[pl.ds((field * extent + target) * sub, reach * sub), :],
                    send_sem=send_sem.at[side, field],
                    recv_sem=recv_sem.at[side, field],
                    device_id=(mem, peer),
                    device_id_type=MESH,
                )
            )
        copies.append(group)
    return copies


def clear_outside(buf, local_rows, sub, lat, size):
    extent = local_rows + 2 * HALO
    zeros = jnp.zeros((HALO * sub, TILE), jnp.float32)

    @pl.when(lat == 0)
    def _():
        for field in range(FIELDS):
            buf[pl.ds(field * extent * sub, HALO * sub), :] = zeros

    @pl.when(lat == size - 1)
    def _():
        for field in range(FIELDS):
            buf[pl.ds((field * extent + HALO + local_rows) * sub, HALO * sub), :] = zeros


def start_halo(copies, lat, size):
    for side, has in ((0, lat > 0), (1, lat < size - 1)):

        @pl.when(has)
        def _(side=side):
            for copy in copies[side]:
                copy.start()


def finish_halo(copies, lat, size):
    for side, has in ((0, lat > 0), (1, lat < size - 1)):

        @pl.when(has)
        def _(side=side):
            for copy in copies[side]:
                copy.wait_send()
            for copy in copies[1 - side]:
                copy.wait_recv()


def planes_from_rows(source, buf, local_rows, sub, fields=range(FIELDS)):
    extent = local_rows + 2 * HALO
    for field in fields:
        for row in range(0, local_rows, 8):
            for t in range(sub):
                first = (field * extent + HALO + row) * sub + t
                buf[pl.ds(first, 8, stride=sub), :] = source[field, row : row + 8, t * TILE : (t + 1) * TILE]


def first_kernel(size, local_rows, sub, x_ref, lab_ref, buf, edge_ref, rows, load_sem, send_sem, recv_sem, lab_send, lab_recv):
    lat = lax.axis_index("lat")
    mem = lax.axis_index("mem")
    barrier = pltpu.get_barrier_semaphore()
    for peer, has in ((lat - 1, lat > 0), (lat + 1, lat < size - 1)):

        @pl.when(has)
        def _(peer=peer):
            pl.semaphore_signal(barrier, inc=1, device_id=(mem, peer), device_id_type=MESH)

    loads = [pltpu.make_async_copy(x_ref.at[f], rows.at[f], load_sem.at[f]) for f in range(FIELDS)]
    for load in loads:
        load.start()
    clear_outside(buf, local_rows, sub, lat, size)
    none = jnp.full((sub, TILE), -1.0, jnp.float32)

    @pl.when(lat == 0)
    def _():
        edge_ref[0] = none

    @pl.when(lat == size - 1)
    def _():
        edge_ref[1] = none

    inner = (lat > 0) & (lat < size - 1)

    @pl.when(inner)
    def _():
        pl.semaphore_wait(barrier, 2)

    @pl.when(jnp.logical_not(inner))
    def _():
        pl.semaphore_wait(barrier, 1)

    copies = halo_copies(buf, local_rows, sub, lat, size, send_sem, recv_sem)
    for side, peer in ((0, lat - 1), (1, lat + 1)):
        row = 0 if side == 0 else local_rows - 1
        copies[side].append(
            pltpu.make_async_remote_copy(
                src_ref=lab_ref.at[row],
                dst_ref=edge_ref.at[1 - side],
                send_sem=lab_send.at[side],
                recv_sem=lab_recv.at[side],
                device_id=(mem, peer),
                device_id_type=MESH,
            )
        )
    for field in range(FIELDS + 1):
        if field < FIELDS:
            loads[field].wait()
            planes_from_rows(rows, buf, local_rows, sub, (field,))
        start_halo([side[field : field + 1] for side in copies], lat, size)
    finish_halo(copies, lat, size)


def second_kernel(
    size, local_rows, sub, first_ref, partner_ref, analysis_ref, lab_ref, edge_ref, buf, factor_ref,
    spread, sums, send_sem, recv_sem, sum_send, sum_recv,
):
    lat = lax.axis_index("lat")
    mem = lax.axis_index("mem")
    extent = local_rows + 2 * HALO
    barrier = pltpu.get_barrier_semaphore()
    for hop in range(1, size):
        pl.semaphore_signal(barrier, inc=1, device_id=(mem, lax.rem(lat + hop, size)), device_id_type=MESH)

    def fold(plane):
        total = plane[0:8]
        for i in range(8, sub, 8):
            total = total + plane[i : i + 8]
        return total

    energies = [jnp.zeros((8, TILE), jnp.float32) for _ in range(REGIONS)]
    counts = [jnp.zeros((8, TILE), jnp.float32) for _ in range(REGIONS)]

    def accumulate(row, carry):
        energies, counts = carry
        total = jnp.zeros((sub, TILE), jnp.float32)
        for field in range(FIELDS):
            parts = []
            for i in range(sub // 8):
                column = ((field * local_rows + row) * (sub // 8) + i) * TILE
                place = pl.ds(pl.multiple_of(column, TILE), TILE)
                parts.append(first_ref[:, place] - partner_ref[:, place])
            half = 0.5 * jnp.concatenate(parts, axis=0)
            spread[field, row] = half
            total = total + half * half
        quarter = 0.125 * total
        here = lab_ref[row]
        before = jnp.where(row == 0, edge_ref[0], lab_ref[jnp.maximum(row - 1, 0)])
        after = jnp.where(row == local_rows - 1, edge_ref[1], lab_ref[jnp.minimum(row + 1, local_rows - 1)])
        new_energies, new_counts = [], []
        for k in range(REGIONS):
            kept = jnp.where(here == k, 1.0, 0.0)
            weight = 2.0 * kept + jnp.where(before == k, 1.0, 0.0) + jnp.where(after == k, 1.0, 0.0)
            new_energies.append(energies[k] + fold(quarter * weight))
            new_counts.append(counts[k] + fold(kept))
        return new_energies, new_counts

    energies, counts = lax.fori_loop(0, local_rows, accumulate, (energies, counts))
    for k in range(REGIONS):
        sums[0, k : k + 1, :] = jnp.sum(energies[k], axis=0, keepdims=True)
        sums[0, REGIONS + k : REGIONS + k + 1, :] = jnp.sum(counts[k], axis=0, keepdims=True)

    pl.semaphore_wait(barrier, size - 1)
    sends = []
    for hop in range(1, size):
        sends.append(
            pltpu.make_async_remote_copy(
                src_ref=sums.at[0],
                dst_ref=sums.at[hop],
                send_sem=sum_send.at[hop],
                recv_sem=sum_recv.at[hop],
                device_id=(mem, lax.rem(lat + hop, size)),
                device_id_type=MESH,
            )
        )
    for copy in sends:
        copy.start()
    clear_outside(buf, local_rows, sub, lat, size)
    planes_from_rows(analysis_ref, buf, local_rows, sub)
    for copy in sends:
        copy.wait()
    total = sums[0]
    for hop in range(1, size):
        total = total + sums[hop]
    total = jnp.sum(total, axis=1, keepdims=True)
    factor = target_size / jnp.sqrt(total[:REGIONS] / total[REGIONS:] + small_eps)
    wide = jnp.broadcast_to(factor, (REGIONS, TILE))
    diagonal = lax.broadcasted_iota(jnp.int32, (REGIONS, TILE), 0) == lax.broadcasted_iota(
        jnp.int32, (REGIONS, TILE), 1
    )
    factor_ref[...] = jnp.sum(jnp.where(diagonal, wide, 0.0), axis=0, keepdims=True)[:, :REGIONS]
    lanes = [jnp.broadcast_to(wide[k : k + 1], (sub, TILE)) for k in range(REGIONS)]

    def middle(row, carry):
        here = lab_ref[row]
        scale = lanes[0]
        for k in range(1, REGIONS):
            scale = jnp.where(here == k, lanes[k], scale)
        for field in range(FIELDS):
            place = pl.ds(pl.multiple_of((field * extent + HALO + row) * sub, sub), sub)
            buf[place, :] = buf[place, :] + scale * spread[field, row]
        return carry

    lax.fori_loop(0, local_rows, middle, 0)
    copies = halo_copies(buf, local_rows, sub, lat, size, send_sem, recv_sem)
    start_halo(copies, lat, size)
    finish_halo(copies, lat, size)


def partner_fields(fields, pairing, index):
    pairs = pairs_of(lax.axis_size("mem"))
    if len(pairs) > MAX_BRANCHES:
        piece = lax.all_gather(fields, "mem", axis=0)
        return lax.dynamic_index_in_dim(piece, pairing[lax.axis_index("mem")], 0, keepdims=False)
    branches = [
        functools.partial(lax.ppermute, axis_name="mem", perm=[(a, b), (b, a)]) for a, b in pairs
    ]
    return lax.switch(index, branches, fields)


def local(replica_variables, analysis, labels, pairing):
    size = lax.axis_size("lat")
    fields, local_rows, width = analysis.shape
    sub = width // TILE
    extent = local_rows + 2 * HALO
    wide = jax.ShapeDtypeStruct((8, fields * local_rows * width // 8), jnp.float32)
    extended = jax.ShapeDtypeStruct((fields * extent * sub, TILE), jnp.float32)
    edges = jax.ShapeDtypeStruct((2, sub, TILE), jnp.float32)
    factors = jax.ShapeDtypeStruct((1, REGIONS), jnp.float32)
    label_planes = jnp.broadcast_to(labels.astype(jnp.float32)[..., None], (local_rows, sub, TILE))
    whole = pl.BlockSpec(memory_space=pltpu.VMEM)
    buffers = [
        pltpu.VMEM((fields * extent * sub, TILE), jnp.float32),
        pltpu.VMEM((extent * sub, TILE), jnp.float32),
    ]
    halo_sems = [pltpu.SemaphoreType.DMA((2, fields)), pltpu.SemaphoreType.DMA((2, fields))]
    state, edge = pl.pallas_call(
        functools.partial(first_kernel, size, local_rows, sub),
        out_shape=(extended, edges),
        in_specs=[pl.BlockSpec(memory_space=pltpu.HBM), whole],
        out_specs=(whole, whole),
        scratch_shapes=[pltpu.VMEM(analysis.shape, jnp.float32), pltpu.SemaphoreType.DMA((fields,))]
        + halo_sems
        + [pltpu.SemaphoreType.DMA((2,)), pltpu.SemaphoreType.DMA((2,))],
        compiler_params=pltpu.CompilerParams(collective_id=0, has_side_effects=True, vmem_limit_bytes=VMEM_LIMIT),
    )(replica_variables[0], label_planes)
    smem = pl.BlockSpec(memory_space=pltpu.SMEM)
    first, index = pl.pallas_call(
        functools.partial(steps_kernel, size, local_rows, sub, False),
        out_shape=(wide, jax.ShapeDtypeStruct((1, 1), jnp.int32)),
        in_specs=[whole, smem],
        out_specs=(whole, smem),
        scratch_shapes=buffers,
        compiler_params=pltpu.CompilerParams(vmem_limit_bytes=VMEM_LIMIT),
    )(state, pairing)
    partner = partner_fields(first, pairing, index[0, 0])
    state, factor = pl.pallas_call(
        functools.partial(second_kernel, size, local_rows, sub),
        out_shape=(extended, factors),
        in_specs=[whole] * 5,
        out_specs=(whole, whole),
        scratch_shapes=[
            pltpu.VMEM((fields, local_rows, sub, TILE), jnp.float32),
            pltpu.VMEM((size, 2 * REGIONS, TILE), jnp.float32),
        ]
        + halo_sems
        + [pltpu.SemaphoreType.DMA((size,)), pltpu.SemaphoreType.DMA((size,))],
        compiler_params=pltpu.CompilerParams(collective_id=1, has_side_effects=True, vmem_limit_bytes=VMEM_LIMIT),
    )(first, partner, analysis, label_planes, edge)
    closing, factor = pl.pallas_call(
        functools.partial(steps_kernel, size, local_rows, sub, True),
        out_shape=(jax.ShapeDtypeStruct(analysis.shape, jnp.float32), factors),
        in_specs=[whole] * 2,
        out_specs=(whole, whole),
        scratch_shapes=buffers,
        compiler_params=pltpu.CompilerParams(vmem_limit_bytes=VMEM_LIMIT),
    )(state, factor)
    return (closing[None], factor)


def solution(mesh):
    return jax.shard_map(
        local,
        mesh=mesh,
        in_specs=(P("mem", None, "lat", None), P(None, "lat", None), P("lat", None), P()),
        out_specs=(P("mem", None, "lat", None), P("mem", None)),
        check_vma=False,
    )
```

profile of v0, /device:TPU:25, one launch (start us, length us, event | category | flops | bytes accessed | tf_op | source)
XLA Modules:
  0.0 77.0 jit_solution(8405308615349411633)
XLA Ops:
  0.6 0.7 convert_element_type.3
  1.3 0.1 broadcast_in_dim.4.lab_ref
  1.5 0.0 copy-start
  1.5 1.2 %copy-done = f32[1,4,16,4096]{3,2,1,0:T(8,128)S(1)} copy-done((f32[1,4,16,4096]{3,2,1,0:T(8,128)S(1)}, f32[1,4,16,4096]{3,2,1,0:T(8,128)}, u32[]{:S(2)}) %copy-start) | copy-done | bytes 1048600
  2.7 0.0 copy-start.1
  2.7 7.0 %shard_map.59 = (f32[3584,128]{1,0:T(8,128)S(1)}, f32[2,32,128]{2,1,0:T(8,128)S(1)}) custom-call(f32[4,16,4096]{2,1,0:T(8,128)S(1)} %bitcast.3, f32[16,32,128]{2,1,0:T(8,128)S(1)} %broadcast_in_dim.4.lab_ref), custom_call_target="tpu_custom_call" | custom-call | tf_op jit(solution)/shard_map/pallas_call | solution.py:370
  9.7 0.0 copy-start.2
  9.7 0.6 copy-done.2
  10.3 2.7 %shard_map.60 = (f32[8,32768]{1,0:T(8,128)S(1)}, s32[1,1]{1,0:T(1,128)}) custom-call(f32[3584,128]{1,0:T(8,128)S(1)} %get-tuple-element.67.refs_0_, s32[8]{0:T(128)S(1)} %copy-done.2), custom_call_target="tpu_custom_call" | custom-call | tf_op jit(solution)/shard_map/pallas_call | solution.py:381
  13.7 48.7 %conditional.1 = (f32[8,32768]{1,0:T(8,128)}) conditional(s32[]{:T(128)} %bitcast.1, f32[8,32768]{1,0:T(8,128)S(1)} %get-tuple-element.68.first_ref, f32[8,32768]{1,0:T(8,128)S(1)} %get-tuple-element.68.first_ref, f32[8,32768]{1,0:T(8,128)S(1)} %get-tuple-element.68.first_ref, ...), branch_computations={%region_0.0_spmd, %region_1.0_spmd, %region_2.0_spmd, %region_3.0_... | conditional | bytes 4194352 | solution.py:351
  13.8 2.9 %collective-permute-start.20 = (f32[8,32768]{1,0:T(8,128)S(1)}, f32[8,32768]{1,0:T(8,128)}, u32[]{:S(2)}, u32[]{:S(2)}) collective-permute-start(f32[8,32768]{1,0:T(8,128)S(1)} %param.20), channel_id=1, source_target_pairs={{12,24},{24,12},{13,25},{25,13},{14,26},{26,14},{15,27},{27,15}} | collective-permute-start | bytes 3145736 | tf_op jit(solution)/shard_map/cond/branch_20_fun/ppermute | solution.py:351
  16.7 45.7 %collective-permute-done.20 = f32[8,32768]{1,0:T(8,128)} collective-permute-done((f32[8,32768]{1,0:T(8,128)S(1)}, f32[8,32768]{1,0:T(8,128)}, u32[]{:S(2)}, u32[]{:S(2)}) %collective-permute-start.20) | collective-permute-done | bytes 1048608 | tf_op jit(solution)/shard_map/cond/branch_20_fun/ppermute | solution.py:351
  62.4 0.0 copy-done.1
  62.4 11.2 %shard_map.61 = (f32[3584,128]{1,0:T(8,128)S(1)}, f32[1,8]{1,0:T(1,128)S(1)}) custom-call(f32[8,32768]{1,0:T(8,128)S(1)} %get-tuple-element.68.first_ref, f32[8,32768]{1,0:T(8,128)} %get-tuple-element.75.partner_ref, f32[4,16,4096]{2,1,0:T(8,128)S(1)} %copy-done.1, f32[16,32,128]{2,1,0:T(8,128)S(1)} %broadcast_in_dim.4.lab_ref, ...), custom_call_target="tpu_custom_call" | custom-call | tf_op jit(solution)/shard_map/pallas_call | solution.py:390
  73.6 3.4 %shard_map.62 = (f32[4,16,4096]{2,1,0:T(8,128)}, f32[1,8]{1,0:T(1,128)}) custom-call(f32[3584,128]{1,0:T(8,128)S(1)} %get-tuple-element.71.refs_0_, f32[1,8]{1,0:T(1,128)S(1)} %get-tuple-element.72.refs_1_), custom_call_target="tpu_custom_call" | custom-call | tf_op jit(solution)/shard_map/pallas_call | solution.py:403
Async XLA Ops:
  1.5 1.2 %copy-start = (f32[1,4,16,4096]{3,2,1,0:T(8,128)S(1)}, f32[1,4,16,4096]{3,2,1,0:T(8,128)}, u32[]{:S(2)}) copy-start(f32[1,4,16,4096]{3,2,1,0:T(8,128)} %param.32) | copy-start | bytes 3145732
  2.7 59.7 %copy-start.1 = (f32[4,16,4096]{2,1,0:T(8,128)S(1)}, f32[4,16,4096]{2,1,0:T(8,128)}, u32[]{:S(2)}) copy-start(f32[4,16,4096]{2,1,0:T(8,128)} %analysis_ref.1) | copy-start | bytes 3145732
  9.7 0.7 copy-start.2
  13.8 48.6 %collective-permute-start.20 = (f32[8,32768]{1,0:T(8,128)S(1)}, f32[8,32768]{1,0:T(8,128)}, u32[]{:S(2)}, u32[]{:S(2)}) collective-permute-start(f32[8,32768]{1,0:T(8,128)S(1)} %param.20), channel_id=1, source_target_pairs={{12,24},{24,12},{13,25},{25,13},{14,26},{26,14},{15,27},{27,15}} | collective-permute-start | bytes 3145736 | tf_op jit(solution)/shard_map/cond/branch_20_fun/ppermute | solution.py:351
where the time goes:
time: 76.5 us; the launch traced here: 77 us
  waiting for transfers between devices  45.7 us (60%)
  Pallas kernels  24.3 us (32%)
  starting transfers between devices  2.92 us (4%)
  local copies, waits for them, and re-layouts  2 us (3%)
  between operations  1.33 us (2%)
    ppermute x1, waiting for transfers between devices, partner_fields(): return lax.switch(index, branches, fields)  45.7 us
    pallas_call x1, Pallas kernels, local(): pl.pallas_call(functools.partial(second_kernel, size, local_rows, sub), o...  11.2 us
    pallas_call x1, Pallas kernels, local(): pl.pallas_call(functools.partial(first_kernel, size, local_rows, sub), ou...  6.98 us
    pallas_call x1, Pallas kernels, local(): pl.pallas_call(functools.partial(steps_kernel, size, local_rows, sub, Tru...  3.4 us
    ppermute x1, starting transfers between devices, partner_fields(): return lax.switch(index, branches, fields)  2.92 us
    pallas_call x1, Pallas kernels, local(): pl.pallas_call(functools.partial(steps_kernel, size, local_rows, sub, Fal...  2.72 us
    unnamed x6, local copies, waits for them, and re-layouts  1.88 us
  transfers between devices with their start and end apart: 1, of which 1 were waited for; matrix products, arithmetic and copies ran while one was open for 0% of the time, Pallas kernels for 0%

commit v1 on v0

--- a/solution.py
+++ b/solution.py
@@ -12,6 +12,8 @@
 REGIONS = 8
 STEPS = 3
 MAX_BRANCHES = 28
+MAX_LEVELS = 4
+OPEN_VMEM = 8 * 2**20
 HALO = 2 * STEPS
 VMEM_LIMIT = 24 * 2**20
 FIELDS = 4
@@ -411,9 +413,520 @@
     return (closing[None], factor)
 
 
+CLASS_ID = 2
+COLUMNS = 2
+CHUNKS = 2
+PAIR_VMEM = 12 * 2**20
+
+
+def matchings(items):
+    if not items:
+        return [()]
+    head, found = items[0], []
+    for i in range(1, len(items)):
+        for rest in matchings(items[1:i] + items[i + 1 :]):
+            found.append(((head, items[i]),) + rest)
+    return found
+
+
+def level_edges(matching):
+    return tuple(sorted(tuple(sorted((a // COLUMNS, b // COLUMNS))) for a, b in matching))
+
+
+def level_patterns(size):
+    return sorted({level_edges(m) for m in matchings(tuple(range(size)))})
+
+
+def slot_tables(edges, levels):
+    peer = [[z, z] for z in range(levels)]
+    slot = [[0, 1] for _ in range(levels)]
+    moves = [0] * levels
+    used = [0] * levels
+    for a, b in edges:
+        if a == b:
+            continue
+        i, j = used[a], used[b]
+        used[a] += 1
+        used[b] += 1
+        peer[a][i], slot[a][i] = b, j
+        peer[b][j], slot[b][j] = a, i
+        moves[a] = moves[b] = 1
+    return peer, slot, moves
+
+
+def pattern_index(patterns, pairing_ref):
+    members = pairing_ref.shape[0]
+    levels = members // COLUMNS
+    level = [lax.div(pairing_ref[m], COLUMNS) for m in range(members)]
+    count = {}
+    for a in range(levels):
+        for b in range(a + 1, levels):
+            count[a, b] = sum(jnp.where(level[a * COLUMNS + i] == b, 1, 0) for i in range(COLUMNS))
+    index = jnp.int32(0)
+    for k, edges in enumerate(patterns):
+        good = None
+        for pair, n in count.items():
+            same = n == sum(e == pair for e in edges)
+            good = same if good is None else good & same
+        index = jnp.where(good, k, index)
+    return index
+
+
+def lookup(index, table):
+    value = jnp.int32(table[0])
+    for k, entry in enumerate(table):
+        if k and entry != table[0]:
+            value = jnp.where(index == k, entry, value)
+    return value
+
+
+def opening_kernel(size, local_rows, sub, x_ref, buf, rows, load_sem, send_sem, recv_sem):
+    lat = lax.axis_index("lat")
+    mem = lax.axis_index("mem")
+    barrier = pltpu.get_barrier_semaphore()
+    for peer, has in ((lat - 1, lat > 0), (lat + 1, lat < size - 1)):
+
+        @pl.when(has)
+        def _(peer=peer):
+            pl.semaphore_signal(barrier, inc=1, device_id=(mem, peer), device_id_type=MESH)
+
+    loads = [pltpu.make_async_copy(x_ref.at[f], rows.at[f], load_sem.at[f]) for f in range(FIELDS)]
+    for load in loads:
+        load.start()
+    clear_outside(buf, local_rows, sub, lat, size)
+    inner = (lat > 0) & (lat < size - 1)
+
+    @pl.when(inner)
+    def _():
+        pl.semaphore_wait(barrier, 2)
+
+    @pl.when(jnp.logical_not(inner))
+    def _():
+        pl.semaphore_wait(barrier, 1)
+
+    copies = halo_copies(buf, local_rows, sub, lat, size, send_sem, recv_sem)
+    for field in range(FIELDS):
+        loads[field].wait()
+        planes_from_rows(rows, buf, local_rows, sub, (field,))
+        start_halo([side[field : field + 1] for side in copies], lat, size)
+    finish_halo(copies, lat, size)
+
+
+def first_steps_kernel(size, local_rows, sub, patterns, state_ref, pairing_ref, out_ref, index_ref, buf, spare):
+    extent = local_rows + 2 * HALO
+    index_ref[0, 0] = pattern_index(patterns, pairing_ref)
+    lat = lax.axis_index("lat")
+    fields = run_steps(state_ref, buf, spare, local_rows, sub, lat * local_rows, local_rows * size)
+    for field, (ref, place) in enumerate(fields):
+        for tile in range(local_rows * sub // 8):
+            out_ref[pl.ds((field * local_rows * sub) + tile * 8, 8), :] = ref[
+                pl.ds((place * extent + HALO) * sub + tile * 8, 8), :
+            ]
+
+
+def plane(sub, index):
+    return pl.ds(pl.multiple_of(index * sub, sub), sub)
+
+
+def fold(block):
+    total = block[0:8]
+    for i in range(8, block.shape[0], 8):
+        total = total + block[i : i + 8]
+    return total
+
+
+def pair_kernel(
+    tables, size, local_rows, sub,
+    first_ref, analysis_ref, lab_ref, pairing_ref,
+    partner, state, labels, weights, tally,
+    av, near, send, came, onward,
+    load_sem, near_send, near_recv, z_send, z_recv, last_send, last_recv,
+    ana_send, ana_recv, lab_send, lab_recv,
+):
+    lat = lax.axis_index("lat")
+    mem = lax.axis_index("mem")
+    z, y = lax.div(mem, COLUMNS), lax.rem(mem, COLUMNS)
+    peer_table, slot_table, moves_table = tables
+    levels = len(moves_table)
+    half = local_rows // COLUMNS
+    deep = half // CHUNKS
+    block = deep * sub
+    chunks = FIELDS * CHUNKS
+    extent = local_rows + 2 * HALO
+    other = (z * COLUMNS + 1 - y, lat)
+    peers = [lookup(z, [peer_table[k][j] for k in range(levels)]) for j in range(2)]
+    slots = [lookup(z, [slot_table[k][j] for k in range(levels)]) for j in range(2)]
+    moves = lookup(z, moves_table) == 1
+
+    load = pltpu.make_async_copy(analysis_ref, av, load_sem.at[0])
+    load.start()
+    barrier = pltpu.get_barrier_semaphore()
+    pl.semaphore_signal(barrier, inc=1, device_id=other, device_id_type=MESH)
+    for hop in range(1, size):
+        pl.semaphore_signal(barrier, inc=1, device_id=(mem, lax.rem(lat + hop, size)), device_id_type=MESH)
+
+    @pl.when(moves)
+    def _():
+        for j in range(2):
+            pl.semaphore_signal(barrier, inc=1, device_id=(peers[j] * COLUMNS + y, lat), device_id_type=MESH)
+
+    @pl.when(moves)
+    def _():
+        pl.semaphore_wait(barrier, size + 2)
+
+    @pl.when(jnp.logical_not(moves))
+    def _():
+        pl.semaphore_wait(barrier, size)
+
+    def rows_of(c, column):
+        field, part = lax.div(c, CHUNKS), lax.rem(c, CHUNKS)
+        return pl.ds(pl.multiple_of((field * local_rows + column * half + part * deep) * sub, sub), block)
+
+    def near_copy(c):
+        return pltpu.make_async_remote_copy(
+            src_ref=first_ref.at[rows_of(c, 1 - y), :],
+            dst_ref=near.at[c],
+            send_sem=near_send.at[c],
+            recv_sem=near_recv.at[c],
+            device_id=other,
+            device_id_type=MESH,
+        )
+
+    def cross_copy(c, j, slot):
+        return pltpu.make_async_remote_copy(
+            src_ref=send.at[j, c],
+            dst_ref=came.at[slot, c],
+            send_sem=z_send.at[j, c],
+            recv_sem=z_recv.at[slot, c],
+            device_id=(peers[j] * COLUMNS + y, lat),
+            device_id_type=MESH,
+        )
+
+    def last_copy(c):
+        return pltpu.make_async_remote_copy(
+            src_ref=onward.at[c],
+            dst_ref=partner.at[rows_of(c, y), :],
+            send_sem=last_send.at[c],
+            recv_sem=last_recv.at[c],
+            device_id=other,
+            device_id_type=MESH,
+        )
+
+    def start_near(c, carry):
+        near_copy(c).start()
+        return carry
+
+    lax.fori_loop(0, chunks, start_near, 0)
+
+    pick = [pairing_ref[z * COLUMNS + i] for i in range(COLUMNS)]
+    pick_level = [lax.div(p, COLUMNS) for p in pick]
+    first_slot_item = jnp.where(pick_level[0] == peers[0], 0, 1)
+    here_level = jnp.where(y == 0, pick_level[0], pick_level[1])
+    here_column = lax.rem(jnp.where(y == 0, pick[0], pick[1]), COLUMNS)
+    keep_slot = jnp.where(peers[0] == peers[1], here_column, jnp.where(here_level == peers[0], 0, 1))
+    own_first = jnp.full((block, TILE), first_slot_item, jnp.int32) == y
+    keep_first = jnp.full((block, TILE), keep_slot, jnp.int32) == 0
+
+    clear_outside(state, local_rows, sub, lat, size)
+    none = jnp.full((HALO * sub, TILE), -1.0, jnp.float32)
+
+    @pl.when(lat == 0)
+    def _():
+        labels[pl.ds(0, HALO * sub), :] = none
+
+    @pl.when(lat == size - 1)
+    def _():
+        labels[pl.ds((HALO + local_rows) * sub, HALO * sub), :] = none
+
+    diagonal = lax.broadcasted_iota(jnp.int32, (sub, sub), 0) == lax.broadcasted_iota(jnp.int32, (sub, sub), 1)
+    load.wait()
+
+    def lay_out(c):
+        for part in range(CHUNKS):
+            block_row = part * 8
+
+            def put(t, carry, block_row=block_row):
+                for i in range(sub // CHUNKS):
+                    tile = lax.rem(c, CHUNKS) * (sub // CHUNKS) + i
+                    field = lax.div(c, CHUNKS)
+                    first = (field * extent + HALO + block_row) * sub + tile
+                    state[pl.ds(first, 8, stride=sub), :] = av[
+                        field, block_row : block_row + 8, pl.ds(pl.multiple_of(tile * TILE, TILE), TILE)
+                    ]
+                return carry
+
+            put(0, 0)
+        for i in range(local_rows // chunks):
+            row = c * (local_rows // chunks) + i
+            line = jnp.broadcast_to(lab_ref[pl.ds(row, 1), :].astype(jnp.float32), (sub, sub))
+            column = jnp.sum(jnp.where(diagonal, line, 0.0), axis=1, keepdims=True)
+            labels[plane(sub, HALO + row), :] = jnp.broadcast_to(column, (sub, TILE))
+
+    def cross(c, carry):
+        lay_out(c)
+        near_copy(c).wait_recv()
+
+        @pl.when(moves)
+        def _():
+            a = first_ref[rows_of(c, y), :]
+            b = near[c]
+            send[0, c] = jnp.where(own_first, a, b)
+            send[1, c] = jnp.where(own_first, b, a)
+            for j in range(2):
+                cross_copy(c, j, slots[j]).start()
+
+        return carry
+
+    lax.fori_loop(0, chunks, cross, 0)
+    ana_copies = halo_copies(state, local_rows, sub, lat, size, ana_send, ana_recv)
+    lab_copies = [
+        [
+            pltpu.make_async_remote_copy(
+                src_ref=labels.at[pl.ds(HALO * sub if side == 0 else local_rows * sub, HALO * sub), :],
+                dst_ref=labels.at[pl.ds((HALO + local_rows) * sub if side == 0 else 0, HALO * sub), :],
+                send_sem=lab_send.at[side],
+                recv_sem=lab_recv.at[side],
+                device_id=(mem, peer),
+                device_id_type=MESH,
+            )
+        ]
+        for side, peer in ((0, lat - 1), (1, lat + 1))
+    ]
+    start_halo(lab_copies, lat, size)
+    start_halo(ana_copies, lat, size)
+
+    def forward(c, carry):
+        @pl.when(moves)
+        def _():
+            for j in range(2):
+                cross_copy(c, j, j).wait()
+            a = came[0, c]
+            b = came[1, c]
+            onward[c] = jnp.where(keep_first, b, a)
+            partner[rows_of(c, y), :] = jnp.where(keep_first, a, b)
+
+        @pl.when(jnp.logical_not(moves))
+        def _():
+            onward[c] = first_ref[rows_of(c, y), :]
+            partner[rows_of(c, y), :] = near[c]
+
+        last_copy(c).start()
+        return carry
+
+    lax.fori_loop(0, chunks, forward, 0)
+    finish_halo(lab_copies, lat, size)
+    finish_halo(ana_copies, lat, size)
+
+    def weigh(row, counts):
+        here = labels[plane(sub, HALO + row), :]
+        before = labels[plane(sub, HALO + row - 1), :]
+        after = labels[plane(sub, HALO + row + 1), :]
+        new = []
+        for k in range(REGIONS):
+            kept = jnp.where(here == k, 1.0, 0.0)
+            around = jnp.where(before == k, 0.125, 0.0) + jnp.where(after == k, 0.125, 0.0)
+            weights[k, plane(sub, row), :] = 0.25 * kept + around
+            new.append(counts[k] + fold(kept))
+        return new
+
+    counts = lax.fori_loop(0, local_rows, weigh, [jnp.zeros((8, TILE), jnp.float32) for _ in range(REGIONS)])
+    for k in range(REGIONS):
+        tally[k : k + 1, :] = jnp.sum(counts[k], axis=0, keepdims=True)
+
+    def finish(c, carry):
+        near_copy(c).wait_send()
+        last_copy(c).wait()
+        return carry
+
+    lax.fori_loop(0, chunks, finish, 0)
+
+
+def rescale_kernel(
+    size, local_rows, sub, first_ref, partner_ref, ana_ref, labels, weights, tally, state, factor_ref,
+    spread, sums, send_sem, recv_sem, sum_send, sum_recv,
+):
+    lat = lax.axis_index("lat")
+    mem = lax.axis_index("mem")
+    extent = local_rows + 2 * HALO
+    barrier = pltpu.get_barrier_semaphore()
+    for hop in range(1, size):
+        pl.semaphore_signal(barrier, inc=1, device_id=(mem, lax.rem(lat + hop, size)), device_id_type=MESH)
+    clear_outside(spread, local_rows, sub, lat, size)
+
+    def accumulate(row, energies):
+        total = jnp.zeros((sub, TILE), jnp.float32)
+        for field in range(FIELDS):
+            there = plane(sub, field * local_rows + row)
+            value = 0.5 * (first_ref[there, :] - partner_ref[there, :])
+            spread[plane(sub, field * extent + HALO + row), :] = value
+            total = total + value * value
+        return [energies[k] + fold(total * weights[k, plane(sub, row), :]) for k in range(REGIONS)]
+
+    energies = [jnp.zeros((8, TILE), jnp.float32) for _ in range(REGIONS)]
+    energies = lax.fori_loop(0, local_rows, accumulate, energies, unroll=2)
+    pl.semaphore_wait(barrier, size - 1)
+    for k in range(REGIONS):
+        sums[0, k : k + 1, :] = jnp.sum(energies[k], axis=0, keepdims=True)
+    sums[0, REGIONS : 2 * REGIONS, :] = tally[...]
+    shares = [
+        pltpu.make_async_remote_copy(
+            src_ref=sums.at[0],
+            dst_ref=sums.at[hop],
+            send_sem=sum_send.at[hop],
+            recv_sem=sum_recv.at[hop],
+            device_id=(mem, lax.rem(lat + hop, size)),
+            device_id_type=MESH,
+        )
+        for hop in range(1, size)
+    ]
+    for copy in shares:
+        copy.start()
+    copies = halo_copies(spread, local_rows, sub, lat, size, send_sem, recv_sem)
+    start_halo(copies, lat, size)
+    for copy in shares:
+        copy.wait()
+    total = sums[0]
+    for hop in range(1, size):
+        total = total + sums[hop]
+    total = jnp.sum(total, axis=1, keepdims=True)
+    factor = target_size / jnp.sqrt(total[:REGIONS] / total[REGIONS:] + small_eps)
+    wide = jnp.broadcast_to(factor, (REGIONS, TILE))
+    diagonal = lax.broadcasted_iota(jnp.int32, (REGIONS, TILE), 0) == lax.broadcasted_iota(
+        jnp.int32, (REGIONS, TILE), 1
+    )
+    factor_ref[...] = jnp.sum(jnp.where(diagonal, wide, 0.0), axis=0, keepdims=True)[:, :REGIONS]
+    lanes = [jnp.broadcast_to(wide[k : k + 1], (sub, TILE)) for k in range(REGIONS)]
+
+    def middle(e, carry):
+        here = labels[plane(sub, e), :]
+        scale = lanes[0]
+        for k in range(1, REGIONS):
+            scale = jnp.where(here == k, lanes[k], scale)
+        for field in range(FIELDS):
+            place = plane(sub, field * extent + e)
+            state[place, :] = ana_ref[place, :] + scale * spread[place, :]
+        return carry
+
+    lax.fori_loop(HALO, HALO + local_rows, middle, 0, unroll=2)
+    finish_halo(copies, lat, size)
+    lax.fori_loop(0, HALO, middle, 0, unroll=2)
+    lax.fori_loop(HALO + local_rows, extent, middle, 0, unroll=2)
+
+
+def pair_call(tables, index, size, fields, local_rows, width):
+    sub = width // TILE
+    half = local_rows // COLUMNS
+    chunks = fields * CHUNKS
+    block = half // CHUNKS * sub
+    extent = local_rows + 2 * HALO
+    f32 = jnp.float32
+    vmem = lambda *shape: pltpu.VMEM(shape, f32)
+    pair = lambda *shape: [pltpu.SemaphoreType.DMA(shape)] * 2
+    whole = pl.BlockSpec(memory_space=pltpu.VMEM)
+    return pl.pallas_call(
+        functools.partial(pair_kernel, tables, size, local_rows, sub),
+        out_shape=(
+            jax.ShapeDtypeStruct((fields * local_rows * sub, TILE), f32),
+            jax.ShapeDtypeStruct((fields * extent * sub, TILE), f32),
+            jax.ShapeDtypeStruct((extent * sub, TILE), f32),
+            jax.ShapeDtypeStruct((REGIONS, local_rows * sub, TILE), f32),
+            jax.ShapeDtypeStruct((REGIONS, TILE), f32),
+        ),
+        in_specs=[whole, pl.BlockSpec(memory_space=pltpu.HBM), whole, pl.BlockSpec(memory_space=pltpu.SMEM)],
+        out_specs=(whole,) * 5,
+        scratch_shapes=[
+            vmem(fields, local_rows, width),
+            vmem(chunks, block, TILE),
+            vmem(2, chunks, block, TILE),
+            vmem(2, chunks, block, TILE),
+            vmem(chunks, block, TILE),
+            pltpu.SemaphoreType.DMA((1,)),
+        ]
+        + pair(chunks)
+        + pair(2, chunks)
+        + pair(chunks)
+        + pair(2, fields)
+        + pair(2),
+        compiler_params=pltpu.CompilerParams(
+            collective_id=CLASS_ID + index, has_side_effects=True, vmem_limit_bytes=PAIR_VMEM
+        ),
+    )
+
+
+def cycle(replica_variables, analysis, labels, pairing):
+    size = lax.axis_size("lat")
+    members = lax.axis_size("mem")
+    fields, local_rows, width = analysis.shape
+    sub = width // TILE
+    extent = local_rows + 2 * HALO
+    extended = jax.ShapeDtypeStruct((fields * extent * sub, TILE), jnp.float32)
+    inner = jax.ShapeDtypeStruct((fields * local_rows * sub, TILE), jnp.float32)
+    factors = jax.ShapeDtypeStruct((1, REGIONS), jnp.float32)
+    patterns = level_patterns(members)
+    whole = pl.BlockSpec(memory_space=pltpu.VMEM)
+    smem = pl.BlockSpec(memory_space=pltpu.SMEM)
+    halo_sems = [pltpu.SemaphoreType.DMA((2, fields)), pltpu.SemaphoreType.DMA((2, fields))]
+    buffers = [
+        pltpu.VMEM((fields * extent * sub, TILE), jnp.float32),
+        pltpu.VMEM((extent * sub, TILE), jnp.float32),
+    ]
+    state = pl.pallas_call(
+        functools.partial(opening_kernel, size, local_rows, sub),
+        out_shape=extended,
+        in_specs=[pl.BlockSpec(memory_space=pltpu.HBM)],
+        out_specs=whole,
+        scratch_shapes=[pltpu.VMEM(analysis.shape, jnp.float32), pltpu.SemaphoreType.DMA((fields,))] + halo_sems,
+        compiler_params=pltpu.CompilerParams(collective_id=0, has_side_effects=True, vmem_limit_bytes=OPEN_VMEM),
+    )(replica_variables[0])
+    first, index = pl.pallas_call(
+        functools.partial(first_steps_kernel, size, local_rows, sub, patterns),
+        out_shape=(inner, jax.ShapeDtypeStruct((1, 1), jnp.int32)),
+        in_specs=[whole, smem],
+        out_specs=(whole, smem),
+        scratch_shapes=buffers,
+        compiler_params=pltpu.CompilerParams(vmem_limit_bytes=PAIR_VMEM),
+    )(state, pairing)
+    branches = [
+        pair_call(slot_tables(edges, members // COLUMNS), k, size, fields, local_rows, width)
+        for k, edges in enumerate(patterns)
+    ]
+    partner, ana, label_planes, weights, tally = lax.switch(index[0, 0], branches, first, analysis, labels, pairing)
+    state, factor = pl.pallas_call(
+        functools.partial(rescale_kernel, size, local_rows, sub),
+        out_shape=(extended, factors),
+        in_specs=[whole] * 6,
+        out_specs=(whole, whole),
+        scratch_shapes=[
+            pltpu.VMEM((fields * extent * sub, TILE), jnp.float32),
+            pltpu.VMEM((size, 2 * REGIONS, TILE), jnp.float32),
+        ]
+        + halo_sems
+        + [pltpu.SemaphoreType.DMA((size,)), pltpu.SemaphoreType.DMA((size,))],
+        compiler_params=pltpu.CompilerParams(collective_id=1, has_side_effects=True, vmem_limit_bytes=PAIR_VMEM),
+    )(first, partner, ana, label_planes, weights, tally)
+    closing, factor = pl.pallas_call(
+        functools.partial(steps_kernel, size, local_rows, sub, True),
+        out_shape=(jax.ShapeDtypeStruct(analysis.shape, jnp.float32), factors),
+        in_specs=[whole] * 2,
+        out_specs=(whole, whole),
+        scratch_shapes=buffers,
+        compiler_params=pltpu.CompilerParams(vmem_limit_bytes=VMEM_LIMIT),
+    )(state, factor)
+    return (closing[None], factor)
+
+
+def either(replica_variables, analysis, labels, pairing):
+    members, rows = lax.axis_size("mem"), analysis.shape[1]
+    levels = members // COLUMNS
+    fits = members % COLUMNS == 0 and 2 <= levels <= MAX_LEVELS
+    if fits and rows == 8 * COLUMNS and rows % (FIELDS * CHUNKS) == 0 and lax.axis_size("lat") > 1:
+        return cycle(replica_variables, analysis, labels, pairing)
+    return local(replica_variables, analysis, labels, pairing)
+
+
 def solution(mesh):
     return jax.shard_map(
-        local,
+        either,
         mesh=mesh,
         in_specs=(P("mem", None, "lat", None), P(None, "lat", None), P("lat", None), P()),
         out_specs=(P("mem", None, "lat", None), P("mem", None)),

time: 76.5 us -> 63.2 us (0.83)
  the two profiles are of different devices: /device:TPU:25 before, /device:TPU:1 now
where the time goes in v1:
time: 63.2 us; the launch traced here: 62.3 us
  Pallas kernels  59.5 us (94%)
  between operations  1.35 us (2%)
  local copies, waits for them, and re-layouts  1.24 us (2%)
    pallas_call x1, Pallas kernels, cycle(): lax.switch(index[0, 0], branches, first, analysis, labels, pairing)  33.6 us
    pallas_call x1, Pallas kernels, cycle(): pl.pallas_call(functools.partial(rescale_kernel, size, local_rows, sub),...  12 us
    pallas_call x1, Pallas kernels, cycle(): pl.pallas_call(functools.partial(opening_kernel, size, local_rows, sub),...  7.58 us
    pallas_call x1, Pallas kernels, cycle(): pl.pallas_call(functools.partial(steps_kernel, size, local_rows, sub, Tru...  3.41 us
    pallas_call x1, Pallas kernels, cycle(): pl.pallas_call(functools.partial(first_steps_kernel, size, local_rows, su...  2.86 us

profile of v1, /device:TPU:1, one launch (start us, length us, event | category | flops | bytes accessed | tf_op | source)
XLA Modules:
  0.0 62.3 jit_solution(546926302310966661)
XLA Ops:
  0.6 0.0 copy-start.3
  0.6 0.0 copy-start
  0.7 1.2 %copy-done = f32[1,4,16,4096]{3,2,1,0:T(8,128)S(1)} copy-done((f32[1,4,16,4096]{3,2,1,0:T(8,128)S(1)}, f32[1,4,16,4096]{3,2,1,0:T(8,128)}, u32[]{:S(2)}) %copy-start) | copy-done | bytes 1048600
  1.9 0.0 copy-start.1
  1.9 0.0 copy-start.2
  1.9 7.6 %shard_map.59.state_ref = f32[3584,128]{1,0:T(8,128)S(1)} custom-call(f32[4,16,4096]{2,1,0:T(8,128)S(1)} %bitcast.3), custom_call_target="tpu_custom_call" | custom-call | tf_op jit(solution)/shard_map/pallas_call | solution.py:873
  9.5 0.0 copy-done.3
  9.5 2.9 %shard_map.60 = (f32[2048,128]{1,0:T(8,128)S(1)}, s32[1,1]{1,0:T(1,128)}) custom-call(f32[3584,128]{1,0:T(8,128)S(1)} %shard_map.59.state_ref, s32[8]{0:T(128)S(1)} %copy-done.3), custom_call_target="tpu_custom_call" | custom-call | tf_op jit(solution)/shard_map/pallas_call | solution.py:881
  13.0 0.0 copy-done.1
  13.0 0.0 copy-done.2
  13.0 33.9 %conditional.1 = ((f32[2048,128]{1,0:T(8,128)S(1)}, f32[3584,128]{1,0:T(8,128)}, f32[896,128]{1,0:T(8,128)}, f32[8,512,128]{2,1,0:T(8,128)}, f32[8,128]{1,0:T(8,128)S(1)})) conditional(s32[]{:T(128)} %bitcast.1, (f32[2048,128]{1,0:T(8,128)S(1)}, f32[4,16,4096]{2,1,0:T(8,128)S(1)}, s32[16,32]{1,0:T(8,128)S(1)}, ...), branch_computations={%region_0.0_spmd, %region_1.0_spmd, %region_2.0_spmd, %region_3.0_... | conditional | bytes 8 | solution.py:893
  13.0 33.6 %branch_6_fun.1 = (f32[2048,128]{1,0:T(8,128)S(1)}, f32[3584,128]{1,0:T(8,128)}, f32[896,128]{1,0:T(8,128)}, f32[8,512,128]{2,1,0:T(8,128)}, f32[8,128]{1,0:T(8,128)S(1)}) custom-call(f32[2048,128]{1,0:T(8,128)S(1)} %get-tuple-element.160.first_ref, f32[4,16,4096]{2,1,0:T(8,128)S(1)} %get-tuple-element.161.analysis_ref, ...), custom_call_target="tpu_custom_call" | custom-call | tf_op jit(solution)/shard_map/cond/branch_6_fun/pallas_call | solution.py:893
  46.9 12.0 %shard_map.61 = (f32[3584,128]{1,0:T(8,128)S(1)}, f32[1,8]{1,0:T(1,128)S(1)}) custom-call(f32[2048,128]{1,0:T(8,128)S(1)} %get-tuple-element.217.first_ref, f32[2048,128]{1,0:T(8,128)S(1)} %get-tuple-element.219.partner_ref, f32[3584,128]{1,0:T(8,128)} %get-tuple-element.220.ana_ref, f32[896,128]{1,0:T(8,128)} %get-tuple-element.221.labels, ...), custom_call_target="tpu_custom_call" | custom-call | tf_op jit(solution)/shard_map/pallas_call | solution.py:894
  58.9 3.4 %shard_map.62 = (f32[4,16,4096]{2,1,0:T(8,128)}, f32[1,8]{1,0:T(1,128)}) custom-call(f32[3584,128]{1,0:T(8,128)S(1)} %get-tuple-element.224.refs_0_, f32[1,8]{1,0:T(1,128)S(1)} %get-tuple-element.225.refs_1_), custom_call_target="tpu_custom_call" | custom-call | tf_op jit(solution)/shard_map/pallas_call | solution.py:907
Async XLA Ops:
  0.6 8.8 %copy-start.3 = (s32[8]{0:T(128)S(1)}, s32[8]{0:T(128)}, u32[]{:S(2)}) copy-start(s32[8]{0:T(128)} %pairing_ref.1) | copy-start | bytes 100
  0.6 1.2 %copy-start = (f32[1,4,16,4096]{3,2,1,0:T(8,128)S(1)}, f32[1,4,16,4096]{3,2,1,0:T(8,128)}, u32[]{:S(2)}) copy-start(f32[1,4,16,4096]{3,2,1,0:T(8,128)} %param.21) | copy-start | bytes 3145732
  1.9 11.1 %copy-start.1 = (f32[4,16,4096]{2,1,0:T(8,128)S(1)}, f32[4,16,4096]{2,1,0:T(8,128)}, u32[]{:S(2)}) copy-start(f32[4,16,4096]{2,1,0:T(8,128)} %param.22) | copy-start | bytes 3145732
  1.9 11.1 %copy-start.2 = (s32[16,32]{1,0:T(8,128)S(1)}, s32[16,32]{1,0:T(8,128)}, u32[]{:S(2)}) copy-start(s32[16,32]{1,0:T(8,128)} %param.23) | copy-start | bytes 6148

commit v2 on v1

--- a/solution.py
+++ b/solution.py
@@ -416,7 +416,7 @@
 CLASS_ID = 2
 COLUMNS = 2
 CHUNKS = 2
-PAIR_VMEM = 12 * 2**20
+PAIR_VMEM = 16 * 2**20
 
 
 def matchings(items):
@@ -538,10 +538,10 @@
 def pair_kernel(
     tables, size, local_rows, sub,
     first_ref, analysis_ref, lab_ref, pairing_ref,
-    partner, state, labels, weights, tally,
-    av, near, send, came, onward,
+    state, factor_ref,
+    av, near, send, came, onward, final, spread, labels, weights, energy, tally, sums,
     load_sem, near_send, near_recv, z_send, z_recv, last_send, last_recv,
-    ana_send, ana_recv, lab_send, lab_recv,
+    ana_send, ana_recv, lab_send, lab_recv, halo_send, halo_recv, sum_send, sum_recv,
 ):
     lat = lax.axis_index("lat")
     mem = lax.axis_index("mem")
@@ -562,13 +562,25 @@
     load.start()
     barrier = pltpu.get_barrier_semaphore()
     pl.semaphore_signal(barrier, inc=1, device_id=other, device_id_type=MESH)
+
+    @pl.when(moves)
+    def _():
+        for j in range(2):
+            pl.semaphore_signal(barrier, inc=1, device_id=(peers[j] * COLUMNS + y, lat), device_id_type=MESH)
+
     for hop in range(1, size):
         pl.semaphore_signal(barrier, inc=1, device_id=(mem, lax.rem(lat + hop, size)), device_id_type=MESH)
-
-    @pl.when(moves)
-    def _():
-        for j in range(2):
-            pl.semaphore_signal(barrier, inc=1, device_id=(peers[j] * COLUMNS + y, lat), device_id_type=MESH)
+    clear_outside(state, local_rows, sub, lat, size)
+    clear_outside(spread, local_rows, sub, lat, size)
+    none = jnp.full((HALO * sub, TILE), -1.0, jnp.float32)
+
+    @pl.when(lat == 0)
+    def _():
+        labels[pl.ds(0, HALO * sub), :] = none
+
+    @pl.when(lat == size - 1)
+    def _():
+        labels[pl.ds((HALO + local_rows) * sub, HALO * sub), :] = none
 
     @pl.when(moves)
     def _():
@@ -605,10 +617,22 @@
     def last_copy(c):
         return pltpu.make_async_remote_copy(
             src_ref=onward.at[c],
-            dst_ref=partner.at[rows_of(c, y), :],
+            dst_ref=final.at[c],
             send_sem=last_send.at[c],
             recv_sem=last_recv.at[c],
             device_id=other,
+            device_id_type=MESH,
+        )
+
+    def halo_copy(field, reach, side, peer):
+        source = HALO if side == 0 else HALO + local_rows - reach
+        target = HALO + local_rows if side == 0 else HALO - reach
+        return pltpu.make_async_remote_copy(
+            src_ref=spread.at[pl.ds(pl.multiple_of((field * extent + source) * sub, sub), reach * sub), :],
+            dst_ref=spread.at[pl.ds(pl.multiple_of((field * extent + target) * sub, sub), reach * sub), :],
+            send_sem=halo_send.at[side, field],
+            recv_sem=halo_recv.at[side, field],
+            device_id=(mem, peer),
             device_id_type=MESH,
         )
 
@@ -624,61 +648,17 @@
     here_level = jnp.where(y == 0, pick_level[0], pick_level[1])
     here_column = lax.rem(jnp.where(y == 0, pick[0], pick[1]), COLUMNS)
     keep_slot = jnp.where(peers[0] == peers[1], here_column, jnp.where(here_level == peers[0], 0, 1))
-    own_first = jnp.full((block, TILE), first_slot_item, jnp.int32) == y
-    keep_first = jnp.full((block, TILE), keep_slot, jnp.int32) == 0
-
-    clear_outside(state, local_rows, sub, lat, size)
-    none = jnp.full((HALO * sub, TILE), -1.0, jnp.float32)
-
-    @pl.when(lat == 0)
-    def _():
-        labels[pl.ds(0, HALO * sub), :] = none
-
-    @pl.when(lat == size - 1)
-    def _():
-        labels[pl.ds((HALO + local_rows) * sub, HALO * sub), :] = none
-
+    own_first = jnp.full((sub, TILE), first_slot_item, jnp.int32) == y
+    keep_first = jnp.full((sub, TILE), keep_slot, jnp.int32) == 0
     diagonal = lax.broadcasted_iota(jnp.int32, (sub, sub), 0) == lax.broadcasted_iota(jnp.int32, (sub, sub), 1)
-    load.wait()
-
-    def lay_out(c):
-        for part in range(CHUNKS):
-            block_row = part * 8
-
-            def put(t, carry, block_row=block_row):
-                for i in range(sub // CHUNKS):
-                    tile = lax.rem(c, CHUNKS) * (sub // CHUNKS) + i
-                    field = lax.div(c, CHUNKS)
-                    first = (field * extent + HALO + block_row) * sub + tile
-                    state[pl.ds(first, 8, stride=sub), :] = av[
-                        field, block_row : block_row + 8, pl.ds(pl.multiple_of(tile * TILE, TILE), TILE)
-                    ]
-                return carry
-
-            put(0, 0)
-        for i in range(local_rows // chunks):
-            row = c * (local_rows // chunks) + i
-            line = jnp.broadcast_to(lab_ref[pl.ds(row, 1), :].astype(jnp.float32), (sub, sub))
-            column = jnp.sum(jnp.where(diagonal, line, 0.0), axis=1, keepdims=True)
-            labels[plane(sub, HALO + row), :] = jnp.broadcast_to(column, (sub, TILE))
-
-    def cross(c, carry):
-        lay_out(c)
-        near_copy(c).wait_recv()
-
-        @pl.when(moves)
-        def _():
-            a = first_ref[rows_of(c, y), :]
-            b = near[c]
-            send[0, c] = jnp.where(own_first, a, b)
-            send[1, c] = jnp.where(own_first, b, a)
-            for j in range(2):
-                cross_copy(c, j, slots[j]).start()
-
+
+    def label_row(row, carry):
+        line = jnp.broadcast_to(lab_ref[pl.ds(row, 1), :].astype(jnp.float32), (sub, sub))
+        column = jnp.sum(jnp.where(diagonal, line, 0.0), axis=1, keepdims=True)
+        labels[plane(sub, HALO + row), :] = jnp.broadcast_to(column, (sub, TILE))
         return carry
 
-    lax.fori_loop(0, chunks, cross, 0)
-    ana_copies = halo_copies(state, local_rows, sub, lat, size, ana_send, ana_recv)
+    lax.fori_loop(0, local_rows, label_row, 0, unroll=4)
     lab_copies = [
         [
             pltpu.make_async_remote_copy(
@@ -693,29 +673,40 @@
         for side, peer in ((0, lat - 1), (1, lat + 1))
     ]
     start_halo(lab_copies, lat, size)
-    start_halo(ana_copies, lat, size)
-
-    def forward(c, carry):
+    load.wait()
+    tiles = FIELDS * sub // chunks
+
+    def lay_out(c):
+        for i in range(tiles):
+            index = c * tiles + i
+            field, tile = lax.div(index, sub), lax.rem(index, sub)
+            for row in range(0, local_rows, 8):
+                state[pl.ds((field * extent + HALO + row) * sub + tile, 8, stride=sub), :] = av[
+                    field, row : row + 8, pl.ds(pl.multiple_of(tile * TILE, TILE), TILE)
+                ]
+
+    def cross(c, carry):
+        near_copy(c).wait_recv()
+
         @pl.when(moves)
         def _():
+            start = rows_of(c, y).start
+            for r in range(deep):
+                here = pl.ds(r * sub, sub)
+                a = first_ref[pl.ds(pl.multiple_of(start + r * sub, sub), sub), :]
+                b = near[c, here, :]
+                send[0, c, here, :] = jnp.where(own_first, a, b)
+                send[1, c, here, :] = jnp.where(own_first, b, a)
             for j in range(2):
-                cross_copy(c, j, j).wait()
-            a = came[0, c]
-            b = came[1, c]
-            onward[c] = jnp.where(keep_first, b, a)
-            partner[rows_of(c, y), :] = jnp.where(keep_first, a, b)
-
-        @pl.when(jnp.logical_not(moves))
-        def _():
-            onward[c] = first_ref[rows_of(c, y), :]
-            partner[rows_of(c, y), :] = near[c]
-
-        last_copy(c).start()
+                cross_copy(c, j, slots[j]).start()
+
+        lay_out(c)
         return carry
 
-    lax.fori_loop(0, chunks, forward, 0)
+    lax.fori_loop(0, chunks, cross, 0)
+    ana_copies = halo_copies(state, local_rows, sub, lat, size, ana_send, ana_recv)
+    start_halo(ana_copies, lat, size)
     finish_halo(lab_copies, lat, size)
-    finish_halo(ana_copies, lat, size)
 
     def weigh(row, counts):
         here = labels[plane(sub, HALO + row), :]
@@ -731,43 +722,80 @@
 
     counts = lax.fori_loop(0, local_rows, weigh, [jnp.zeros((8, TILE), jnp.float32) for _ in range(REGIONS)])
     for k in range(REGIONS):
-        tally[k : k + 1, :] = jnp.sum(counts[k], axis=0, keepdims=True)
-
-    def finish(c, carry):
-        near_copy(c).wait_send()
-        last_copy(c).wait()
+        tally[pl.ds(k * 8, 8), :] = counts[k]
+    energy[...] = jnp.zeros_like(energy)
+
+    def absorb(field, first_row, theirs):
+        totals = [energy[pl.ds(k * 8, 8), :] for k in range(REGIONS)]
+        for r in range(deep):
+            row = first_row + r
+            value = 0.5 * (first_ref[plane(sub, field * local_rows + row), :] - theirs[r * sub : (r + 1) * sub, :])
+            spread[plane(sub, field * extent + HALO + row), :] = value
+            square = value * value
+            for k in range(REGIONS):
+                totals[k] = totals[k] + fold(square * weights[k, plane(sub, row), :])
+        for k in range(REGIONS):
+            energy[pl.ds(k * 8, 8), :] = totals[k]
+
+    def forward(field, part):
+        c = field * CHUNKS + part
+
+        @pl.when(moves)
+        def _():
+            for j in range(2):
+                cross_copy(c, j, j).wait_recv()
+            for r in range(deep):
+                here = pl.ds(r * sub, sub)
+                a = came[0, c, here, :]
+                b = came[1, c, here, :]
+                onward[c, here, :] = jnp.where(keep_first, b, a)
+                near[c, here, :] = jnp.where(keep_first, a, b)
+
+        @pl.when(jnp.logical_not(moves))
+        def _():
+            onward[c] = first_ref[rows_of(c, y), :]
+
+        last_copy(c).start()
+
+        absorb(field, y * half + part * deep, near.at[c])
+
+    def arrive(field, part):
+        c = field * CHUNKS + part
+        last_copy(c).wait_recv()
+        absorb(field, (1 - y) * half + part * deep, final.at[c])
+
+    sides = ((0, lat - 1, lat > 0), (1, lat + 1, lat < size - 1))
+
+    def send_halo(field, reach):
+        for side, peer, has in sides:
+
+            @pl.when(has)
+            def _(side=side, peer=peer):
+                halo_copy(field, reach, side, peer).start()
+
+    def stage(c, carry):
+        @pl.when(c < chunks)
+        def _():
+            forward(lax.div(c, CHUNKS), lax.rem(c, CHUNKS))
+
+        @pl.when(c > 0)
+        def _():
+            field, part = lax.div(c - 1, CHUNKS), lax.rem(c - 1, CHUNKS)
+            arrive(field, part)
+
+            @pl.when((part == CHUNKS - 1) & (field < FIELDS - 1))
+            def _():
+                send_halo(field, HALO)
+
         return carry
 
-    lax.fori_loop(0, chunks, finish, 0)
-
-
-def rescale_kernel(
-    size, local_rows, sub, first_ref, partner_ref, ana_ref, labels, weights, tally, state, factor_ref,
-    spread, sums, send_sem, recv_sem, sum_send, sum_recv,
-):
-    lat = lax.axis_index("lat")
-    mem = lax.axis_index("mem")
-    extent = local_rows + 2 * HALO
-    barrier = pltpu.get_barrier_semaphore()
-    for hop in range(1, size):
-        pl.semaphore_signal(barrier, inc=1, device_id=(mem, lax.rem(lat + hop, size)), device_id_type=MESH)
-    clear_outside(spread, local_rows, sub, lat, size)
-
-    def accumulate(row, energies):
-        total = jnp.zeros((sub, TILE), jnp.float32)
-        for field in range(FIELDS):
-            there = plane(sub, field * local_rows + row)
-            value = 0.5 * (first_ref[there, :] - partner_ref[there, :])
-            spread[plane(sub, field * extent + HALO + row), :] = value
-            total = total + value * value
-        return [energies[k] + fold(total * weights[k, plane(sub, row), :]) for k in range(REGIONS)]
-
-    energies = [jnp.zeros((8, TILE), jnp.float32) for _ in range(REGIONS)]
-    energies = lax.fori_loop(0, local_rows, accumulate, energies, unroll=2)
-    pl.semaphore_wait(barrier, size - 1)
+    lax.fori_loop(0, chunks + 1, stage, 0)
+    send_halo(FIELDS - 1, REACH[FIELDS - 1])
     for k in range(REGIONS):
-        sums[0, k : k + 1, :] = jnp.sum(energies[k], axis=0, keepdims=True)
-    sums[0, REGIONS : 2 * REGIONS, :] = tally[...]
+        for i, table in enumerate((energy, tally)):
+            sums[0, i * REGIONS + k : i * REGIONS + k + 1, :] = jnp.sum(
+                table[pl.ds(k * 8, 8), :], axis=0, keepdims=True
+            )
     shares = [
         pltpu.make_async_remote_copy(
             src_ref=sums.at[0],
@@ -781,8 +809,20 @@
     ]
     for copy in shares:
         copy.start()
-    copies = halo_copies(spread, local_rows, sub, lat, size, send_sem, recv_sem)
-    start_halo(copies, lat, size)
+    finish_halo(ana_copies, lat, size)
+
+    def finish(c, carry):
+        near_copy(c).wait_send()
+        last_copy(c).wait_send()
+
+        @pl.when(moves)
+        def _():
+            for j in range(2):
+                cross_copy(c, j, j).wait_send()
+
+        return carry
+
+    lax.fori_loop(0, chunks, finish, 0)
     for copy in shares:
         copy.wait()
     total = sums[0]
@@ -791,10 +831,10 @@
     total = jnp.sum(total, axis=1, keepdims=True)
     factor = target_size / jnp.sqrt(total[:REGIONS] / total[REGIONS:] + small_eps)
     wide = jnp.broadcast_to(factor, (REGIONS, TILE))
-    diagonal = lax.broadcasted_iota(jnp.int32, (REGIONS, TILE), 0) == lax.broadcasted_iota(
+    corner = lax.broadcasted_iota(jnp.int32, (REGIONS, TILE), 0) == lax.broadcasted_iota(
         jnp.int32, (REGIONS, TILE), 1
     )
-    factor_ref[...] = jnp.sum(jnp.where(diagonal, wide, 0.0), axis=0, keepdims=True)[:, :REGIONS]
+    factor_ref[...] = jnp.sum(jnp.where(corner, wide, 0.0), axis=0, keepdims=True)[:, :REGIONS]
     lanes = [jnp.broadcast_to(wide[k : k + 1], (sub, TILE)) for k in range(REGIONS)]
 
     def middle(e, carry):
@@ -804,13 +844,19 @@
             scale = jnp.where(here == k, lanes[k], scale)
         for field in range(FIELDS):
             place = plane(sub, field * extent + e)
-            state[place, :] = ana_ref[place, :] + scale * spread[place, :]
+            state[place, :] = state[place, :] + scale * spread[place, :]
         return carry
 
-    lax.fori_loop(HALO, HALO + local_rows, middle, 0, unroll=2)
-    finish_halo(copies, lat, size)
-    lax.fori_loop(0, HALO, middle, 0, unroll=2)
-    lax.fori_loop(HALO + local_rows, extent, middle, 0, unroll=2)
+    for field in range(FIELDS):
+        reach = REACH[field] if field == FIELDS - 1 else HALO
+        for side, peer, has in sides:
+
+            @pl.when(has)
+            def _(field=field, reach=reach, side=side, peer=peer):
+                halo_copy(field, reach, side, peer).wait_send()
+                halo_copy(field, reach, 1 - side, peer).wait_recv()
+
+    lax.fori_loop(0, extent, middle, 0, unroll=2)
 
 
 def pair_call(tables, index, size, fields, local_rows, width):
@@ -826,27 +872,33 @@
     return pl.pallas_call(
         functools.partial(pair_kernel, tables, size, local_rows, sub),
         out_shape=(
-            jax.ShapeDtypeStruct((fields * local_rows * sub, TILE), f32),
             jax.ShapeDtypeStruct((fields * extent * sub, TILE), f32),
-            jax.ShapeDtypeStruct((extent * sub, TILE), f32),
-            jax.ShapeDtypeStruct((REGIONS, local_rows * sub, TILE), f32),
-            jax.ShapeDtypeStruct((REGIONS, TILE), f32),
+            jax.ShapeDtypeStruct((1, REGIONS), f32),
         ),
         in_specs=[whole, pl.BlockSpec(memory_space=pltpu.HBM), whole, pl.BlockSpec(memory_space=pltpu.SMEM)],
-        out_specs=(whole,) * 5,
+        out_specs=(whole, whole),
         scratch_shapes=[
             vmem(fields, local_rows, width),
             vmem(chunks, block, TILE),
             vmem(2, chunks, block, TILE),
             vmem(2, chunks, block, TILE),
             vmem(chunks, block, TILE),
+            vmem(chunks, block, TILE),
+            vmem(fields * extent * sub, TILE),
+            vmem(extent * sub, TILE),
+            vmem(REGIONS, local_rows * sub, TILE),
+            vmem(REGIONS * 8, TILE),
+            vmem(REGIONS * 8, TILE),
+            vmem(size, 2 * REGIONS, TILE),
             pltpu.SemaphoreType.DMA((1,)),
         ]
         + pair(chunks)
         + pair(2, chunks)
         + pair(chunks)
         + pair(2, fields)
-        + pair(2),
+        + pair(2)
+        + pair(2, fields)
+        + pair(size),
         compiler_params=pltpu.CompilerParams(
             collective_id=CLASS_ID + index, has_side_effects=True, vmem_limit_bytes=PAIR_VMEM
         ),
@@ -877,7 +929,7 @@
         out_specs=whole,
         scratch_shapes=[pltpu.VMEM(analysis.shape, jnp.float32), pltpu.SemaphoreType.DMA((fields,))] + halo_sems,
         compiler_params=pltpu.CompilerParams(collective_id=0, has_side_effects=True, vmem_limit_bytes=OPEN_VMEM),
-    )(replica_variables[0])
+    )(pltpu.with_memory_space_constraint(replica_variables[0], pltpu.HBM))
     first, index = pl.pallas_call(
         functools.partial(first_steps_kernel, size, local_rows, sub, patterns),
         out_shape=(inner, jax.ShapeDtypeStruct((1, 1), jnp.int32)),
@@ -890,20 +942,9 @@
         pair_call(slot_tables(edges, members // COLUMNS), k, size, fields, local_rows, width)
         for k, edges in enumerate(patterns)
     ]
-    partner, ana, label_planes, weights, tally = lax.switch(index[0, 0], branches, first, analysis, labels, pairing)
-    state, factor = pl.pallas_call(
-        functools.partial(rescale_kernel, size, local_rows, sub),
-        out_shape=(extended, factors),
-        in_specs=[whole] * 6,
-        out_specs=(whole, whole),
-        scratch_shapes=[
-            pltpu.VMEM((fields * extent * sub, TILE), jnp.float32),
-            pltpu.VMEM((size, 2 * REGIONS, TILE), jnp.float32),
-        ]
-        + halo_sems
-        + [pltpu.SemaphoreType.DMA((size,)), pltpu.SemaphoreType.DMA((size,))],
-        compiler_params=pltpu.CompilerParams(collective_id=1, has_side_effects=True, vmem_limit_bytes=PAIR_VMEM),
-    )(first, partner, ana, label_planes, weights, tally)
+    state, factor = lax.switch(
+        index[0, 0], branches, first, pltpu.with_memory_space_constraint(analysis, pltpu.HBM), labels, pairing
+    )
     closing, factor = pl.pallas_call(
         functools.partial(steps_kernel, size, local_rows, sub, True),
         out_shape=(jax.ShapeDtypeStruct(analysis.shape, jnp.float32), factors),

time: 63.2 us -> 55.4 us (0.88)
  Pallas kernels: 59.5 us -> 52.9 us
  local copies, waits for them, and re-layouts: 1.24 us -> 0.01 us
    pallas_call x2 -> x1, Pallas kernels: 45.7 us -> 38.3 us  [cycle(): lax.switch(index[0, 0], branches, first, pltpu.with_memory_space_constrai...]
    unnamed x8 -> x4, local copies, waits for them, and re-layouts: 1.24 us -> 0.01 us
    pallas_call x1, Pallas kernels: 7.58 us -> 8.47 us  [cycle(): pl.pallas_call(functools.partial(opening_kernel, size, local_rows, sub),...]
where the time goes in v2:
time: 55.4 us; the launch traced here: 54.7 us
  Pallas kernels  52.9 us (95%)
  between operations  1.33 us (2%)
    pallas_call x1, Pallas kernels, cycle(): lax.switch(index[0, 0], branches, first, pltpu.with_memory_space_constrai...  38.3 us
    pallas_call x1, Pallas kernels, cycle(): pl.pallas_call(functools.partial(opening_kernel, size, local_rows, sub),...  8.47 us
    pallas_call x1, Pallas kernels, cycle(): pl.pallas_call(functools.partial(steps_kernel, size, local_rows, sub, Tru...  3.42 us
    pallas_call x1, Pallas kernels, cycle(): pl.pallas_call(functools.partial(first_steps_kernel, size, local_rows, su...  2.77 us

profile of v2, /device:TPU:1, one launch (start us, length us, event | category | flops | bytes accessed | tf_op | source)
XLA Modules:
  0.0 54.7 jit_solution(4795615440470901089)
XLA Ops:
  0.6 0.0 copy-start.1
  0.6 0.0 copy-start
  0.6 8.5 %shard_map.59.state_ref = f32[3584,128]{1,0:T(8,128)S(1)} custom-call(f32[4,16,4096]{2,1,0:T(8,128)} %bitcast.3), custom_call_target="tpu_custom_call" | custom-call | tf_op jit(solution)/shard_map/pallas_call | solution.py:925
  9.1 0.0 copy-done.1
  9.1 2.8 %shard_map.60 = (f32[2048,128]{1,0:T(8,128)S(1)}, s32[1,1]{1,0:T(1,128)}) custom-call(f32[3584,128]{1,0:T(8,128)S(1)} %shard_map.59.state_ref, s32[8]{0:T(128)S(1)} %copy-done.1), custom_call_target="tpu_custom_call" | custom-call | tf_op jit(solution)/shard_map/pallas_call | solution.py:933
  12.6 0.0 copy-done
  12.6 38.8 %conditional.1 = ((f32[3584,128]{1,0:T(8,128)S(1)}, f32[1,8]{1,0:T(1,128)S(1)})) conditional(s32[]{:T(128)} %bitcast.1, (f32[2048,128]{1,0:T(8,128)S(1)}, f32[4,16,4096]{2,1,0:T(8,128)}, s32[16,32]{1,0:T(8,128)S(1)}, s32[8]{0:T(128)S(1)}) %tuple.112, (f32[2048,128]{1,0:T(8,128)S(1)}, f32[4,16,4096]{2,1,0:T(8,128)}, ...), branch_computations={%region_0.0_spmd, %region_1.0_spmd, %region_2.0_spmd, %region_3.0_... | conditional | bytes 8 | solution.py:945
  12.6 38.3 %branch_9_fun.1 = (f32[3584,128]{1,0:T(8,128)S(1)}, f32[1,8]{1,0:T(1,128)S(1)}) custom-call(f32[2048,128]{1,0:T(8,128)S(1)} %get-tuple-element.172.first_ref, f32[4,16,4096]{2,1,0:T(8,128)} %get-tuple-element.173.analysis_ref, s32[16,32]{1,0:T(8,128)S(1)} %get-tuple-element.174.lab_ref, s32[8]{0:T(128)S(1)} %get-tuple-element.175.pairing_ref), custom_call_target="tpu_custom_call" | custom-call | tf_op jit(solution)/shard_map/cond/branch_9_fun/pallas_call | solution.py:945
  51.3 3.4 %shard_map.61 = (f32[4,16,4096]{2,1,0:T(8,128)}, f32[1,8]{1,0:T(1,128)}) custom-call(f32[3584,128]{1,0:T(8,128)S(1)} %get-tuple-element.214.refs_0_, f32[1,8]{1,0:T(1,128)S(1)} %get-tuple-element.215.refs_1_), custom_call_target="tpu_custom_call" | custom-call | tf_op jit(solution)/shard_map/pallas_call | solution.py:948
Async XLA Ops:
  0.6 8.5 %copy-start.1 = (s32[8]{0:T(128)S(1)}, s32[8]{0:T(128)}, u32[]{:S(2)}) copy-start(s32[8]{0:T(128)} %pairing_ref.1) | copy-start | bytes 100
  0.6 11.9 %copy-start = (s32[16,32]{1,0:T(8,128)S(1)}, s32[16,32]{1,0:T(8,128)}, u32[]{:S(2)}) copy-start(s32[16,32]{1,0:T(8,128)} %param.23) | copy-start | bytes 6148

commit v3 on v2

--- a/solution.py
+++ b/solution.py
@@ -13,7 +13,6 @@
 STEPS = 3
 MAX_BRANCHES = 28
 MAX_LEVELS = 4
-OPEN_VMEM = 8 * 2**20
 HALO = 2 * STEPS
 VMEM_LIMIT = 24 * 2**20
 FIELDS = 4
@@ -414,6 +413,7 @@
 
 
 CLASS_ID = 2
+ORDER = (2, 1, 0, 3)
 COLUMNS = 2
 CHUNKS = 2
 PAIR_VMEM = 16 * 2**20
@@ -480,7 +480,106 @@
     return value
 
 
-def opening_kernel(size, local_rows, sub, x_ref, buf, rows, load_sem, send_sem, recv_sem):
+class Flow:
+    def __init__(self, local_rows, sub, start, rows_all):
+        self.local_rows, self.sub, self.start, self.rows_all = local_rows, sub, start, rows_all
+        self.extent = local_rows + 2 * HALO
+
+    def at(self, field, e):
+        return pl.ds((field * self.extent + e) * self.sub, self.sub)
+
+    def owns(self, e):
+        return HALO <= e < HALO + self.local_rows
+
+    def masked(self, e, values):
+        if self.owns(e):
+            return values
+        row = self.start + (e - HALO)
+        return jnp.where((row >= 0) & (row < self.rows_all), 1.0, 0.0).astype(jnp.float32) * values
+
+    def height(self, source, e):
+        divergence = diff_lon(source[self.at(1, e), :]) + source[self.at(2, e + 1), :] - source[self.at(2, e - 1), :]
+        return self.masked(e, source[self.at(0, e), :] - depth_coef * divergence)
+
+    def wind(self, source, heights, e):
+        row = (self.start + (e - HALO)).astype(jnp.float32)
+        f = coriolis_coef * (2.0 * (row + 0.5) / self.rows_all - 1.0)
+        v = source[self.at(2, e), :]
+        u1 = source[self.at(1, e), :] + f * v - grav_coef * diff_lon(heights[self.at(0, e), :])
+        slope = heights[self.at(0, e + 1), :] - heights[self.at(0, e - 1), :]
+        return u1, self.masked(e, v - f * u1 - grav_coef * slope)
+
+    def tracer(self, source, place, u1, v1, e):
+        q = source[self.at(place, e), :]
+        upper, lower = source[self.at(place, e + 1), :], source[self.at(place, e - 1), :]
+        east, west = shift_lon(q)
+        advected = u1 * (east - west) + v1 * (upper - lower)
+        spreading = east + west + upper + lower - 4.0 * q
+        return self.masked(e, q - advect_coef * advected + diffuse_coef * spreading)
+
+
+def flow_steps(flow, state, buf, spare, keep, flow_halo, tracer_halo, flow_done):
+    low, high = HALO, HALO + flow.local_rows
+    source, place, tracer_source = state, 3, state
+    for step in range(STEPS):
+        margin = 2 * (STEPS - 1 - step)
+        narrow = STEPS - 1 - step
+        last = step == STEPS - 1
+        target, spot = (spare, 0) if step % 2 == 0 else (buf, 3)
+
+        def heights(rows, source=source, last=last):
+            for e in rows:
+                value = flow.height(source, e)
+                buf[flow.at(0, e), :] = value
+                if last and keep is not None and flow.owns(e):
+                    keep(0, e, value)
+
+        def winds(rows, source=source, last=last):
+            for e in rows:
+                u1, v1 = flow.wind(source, buf, e)
+                buf[flow.at(1, e), :] = u1
+                buf[flow.at(2, e), :] = v1
+                if last and keep is not None:
+                    keep(1, e, u1)
+                    keep(2, e, v1)
+
+        def tracers(rows, last=last, tracer_source=tracer_source, place=place, target=target, spot=spot):
+            for e in rows:
+                value = flow.tracer(tracer_source, place, buf[flow.at(1, e), :], buf[flow.at(2, e), :], e)
+                if last and keep is not None:
+                    keep(3, e, value)
+                else:
+                    target[flow.at(spot, e), :] = value
+
+        def run(piece, lower, upper, inner):
+            if inner is None:
+                piece(range(lower, upper))
+            else:
+                piece(range(lower, inner[0]))
+                piece(range(inner[1], upper))
+
+        early = step == 0 and flow_halo is not None
+        inner = [None] * 3
+        if early:
+            inner = [(low + 1, high - 1), (low + 2, high - 2), (low + 2, high - 2)]
+            for piece, rows in zip((heights, winds, tracers), inner):
+                piece(range(*rows))
+            flow_halo()
+        run(heights, low - margin - 1, high + margin + 1, inner[0])
+        run(winds, low - margin, high + margin, inner[1])
+        if early:
+            tracer_halo()
+        if last and flow_done is not None:
+            flow_done()
+        run(tracers, low - narrow, high + narrow, inner[2])
+        source, tracer_source, place = buf, target, spot
+    return tracer_source, place
+
+
+def opening_kernel(
+    size, local_rows, sub, patterns, x_ref, pairing_ref, out_ref, index_ref,
+    state, buf, spare, rows, load_sem, send_sem, recv_sem,
+):
     lat = lax.axis_index("lat")
     mem = lax.axis_index("mem")
     barrier = pltpu.get_barrier_semaphore()
@@ -491,9 +590,10 @@
             pl.semaphore_signal(barrier, inc=1, device_id=(mem, peer), device_id_type=MESH)
 
     loads = [pltpu.make_async_copy(x_ref.at[f], rows.at[f], load_sem.at[f]) for f in range(FIELDS)]
-    for load in loads:
-        load.start()
-    clear_outside(buf, local_rows, sub, lat, size)
+    for f in ORDER:
+        loads[f].start()
+    index_ref[0, 0] = pattern_index(patterns, pairing_ref)
+    clear_outside(state, local_rows, sub, lat, size)
     inner = (lat > 0) & (lat < size - 1)
 
     @pl.when(inner)
@@ -504,24 +604,31 @@
     def _():
         pl.semaphore_wait(barrier, 1)
 
-    copies = halo_copies(buf, local_rows, sub, lat, size, send_sem, recv_sem)
-    for field in range(FIELDS):
-        loads[field].wait()
-        planes_from_rows(rows, buf, local_rows, sub, (field,))
-        start_halo([side[field : field + 1] for side in copies], lat, size)
-    finish_halo(copies, lat, size)
-
-
-def first_steps_kernel(size, local_rows, sub, patterns, state_ref, pairing_ref, out_ref, index_ref, buf, spare):
-    extent = local_rows + 2 * HALO
-    index_ref[0, 0] = pattern_index(patterns, pairing_ref)
-    lat = lax.axis_index("lat")
-    fields = run_steps(state_ref, buf, spare, local_rows, sub, lat * local_rows, local_rows * size)
-    for field, (ref, place) in enumerate(fields):
-        for tile in range(local_rows * sub // 8):
-            out_ref[pl.ds((field * local_rows * sub) + tile * 8, 8), :] = ref[
-                pl.ds((place * extent + HALO) * sub + tile * 8, 8), :
-            ]
+    copies = halo_copies(state, local_rows, sub, lat, size, send_sem, recv_sem)
+    for f in ORDER:
+        loads[f].wait()
+        planes_from_rows(rows, state, local_rows, sub, (f,))
+        start_halo([side[f : f + 1] for side in copies], lat, size)
+
+    def received(fields):
+        for side, has in ((0, lat > 0), (1, lat < size - 1)):
+
+            @pl.when(has)
+            def _(side=side):
+                for f in fields:
+                    copies[1 - side][f].wait_recv()
+
+    def keep(field, e, value):
+        out_ref[pl.ds((field * local_rows + e - HALO) * sub, sub), :] = value
+
+    flow = Flow(local_rows, sub, lat * local_rows, local_rows * size)
+    flow_steps(flow, state, buf, spare, keep, lambda: received(ORDER[:3]), lambda: received(ORDER[3:]), None)
+    for side, has in ((0, lat > 0), (1, lat < size - 1)):
+
+        @pl.when(has)
+        def _(side=side):
+            for copy in copies[side]:
+                copy.wait_send()
 
 
 def plane(sub, index):
@@ -790,7 +897,6 @@
         return carry
 
     lax.fori_loop(0, chunks + 1, stage, 0)
-    send_halo(FIELDS - 1, REACH[FIELDS - 1])
     for k in range(REGIONS):
         for i, table in enumerate((energy, tally)):
             sums[0, i * REGIONS + k : i * REGIONS + k + 1, :] = jnp.sum(
@@ -809,6 +915,7 @@
     ]
     for copy in shares:
         copy.start()
+    send_halo(FIELDS - 1, REACH[FIELDS - 1])
     finish_halo(ana_copies, lat, size)
 
     def finish(c, carry):
@@ -847,6 +954,7 @@
             state[place, :] = state[place, :] + scale * spread[place, :]
         return carry
 
+    lax.fori_loop(HALO, HALO + local_rows, middle, 0, unroll=2)
     for field in range(FIELDS):
         reach = REACH[field] if field == FIELDS - 1 else HALO
         for side, peer, has in sides:
@@ -856,7 +964,8 @@
                 halo_copy(field, reach, side, peer).wait_send()
                 halo_copy(field, reach, 1 - side, peer).wait_recv()
 
-    lax.fori_loop(0, extent, middle, 0, unroll=2)
+    lax.fori_loop(0, HALO, middle, 0, unroll=2)
+    lax.fori_loop(HALO + local_rows, extent, middle, 0, unroll=2)
 
 
 def pair_call(tables, index, size, fields, local_rows, width):
@@ -911,7 +1020,6 @@
     fields, local_rows, width = analysis.shape
     sub = width // TILE
     extent = local_rows + 2 * HALO
-    extended = jax.ShapeDtypeStruct((fields * extent * sub, TILE), jnp.float32)
     inner = jax.ShapeDtypeStruct((fields * local_rows * sub, TILE), jnp.float32)
     factors = jax.ShapeDtypeStruct((1, REGIONS), jnp.float32)
     patterns = level_patterns(members)
@@ -922,22 +1030,17 @@
         pltpu.VMEM((fields * extent * sub, TILE), jnp.float32),
         pltpu.VMEM((extent * sub, TILE), jnp.float32),
     ]
-    state = pl.pallas_call(
-        functools.partial(opening_kernel, size, local_rows, sub),
-        out_shape=extended,
-        in_specs=[pl.BlockSpec(memory_space=pltpu.HBM)],
-        out_specs=whole,
-        scratch_shapes=[pltpu.VMEM(analysis.shape, jnp.float32), pltpu.SemaphoreType.DMA((fields,))] + halo_sems,
-        compiler_params=pltpu.CompilerParams(collective_id=0, has_side_effects=True, vmem_limit_bytes=OPEN_VMEM),
-    )(pltpu.with_memory_space_constraint(replica_variables[0], pltpu.HBM))
     first, index = pl.pallas_call(
-        functools.partial(first_steps_kernel, size, local_rows, sub, patterns),
+        functools.partial(opening_kernel, size, local_rows, sub, patterns),
         out_shape=(inner, jax.ShapeDtypeStruct((1, 1), jnp.int32)),
-        in_specs=[whole, smem],
+        in_specs=[pl.BlockSpec(memory_space=pltpu.HBM), smem],
         out_specs=(whole, smem),
-        scratch_shapes=buffers,
-        compiler_params=pltpu.CompilerParams(vmem_limit_bytes=PAIR_VMEM),
-    )(state, pairing)
+        scratch_shapes=[pltpu.VMEM((fields * extent * sub, TILE), jnp.float32)]
+        + buffers
+        + [pltpu.VMEM(analysis.shape, jnp.float32), pltpu.SemaphoreType.DMA((fields,))]
+        + halo_sems,
+        compiler_params=pltpu.CompilerParams(collective_id=0, has_side_effects=True, vmem_limit_bytes=PAIR_VMEM),
+    )(pltpu.with_memory_space_constraint(replica_variables[0], pltpu.HBM), pairing)
     branches = [
         pair_call(slot_tables(edges, members // COLUMNS), k, size, fields, local_rows, width)
         for k, edges in enumerate(patterns)

time: 55.4 us -> 75.4 us (1.36)
  the two profiles are of different devices: /device:TPU:1 before, /device:TPU:11 now
where the time goes in v3:
time: 75.4 us; the launch traced here: 74.8 us
  Pallas kernels  73 us (97%)
  between operations  1.26 us (2%)
    pallas_call x1, Pallas kernels, cycle(): lax.switch(index[0, 0], branches, first, pltpu.with_memory_space_constrai...  64.1 us
    pallas_call x1, Pallas kernels, cycle(): pl.pallas_call(functools.partial(opening_kernel, size, local_rows, sub, p...  5.65 us
    pallas_call x1, Pallas kernels, cycle(): pl.pallas_call(functools.partial(steps_kernel, size, local_rows, sub, Tru...  3.33 us

profile of v3, /device:TPU:11, one launch (start us, length us, event | category | flops | bytes accessed | tf_op | source)
XLA Modules:
  0.0 74.8 jit_solution(7591541682903344789)
XLA Ops:
  0.6 5.7 %shard_map.59 = (f32[2048,128]{1,0:T(8,128)S(1)}, s32[1,1]{1,0:T(1,128)}) custom-call(f32[4,16,4096]{2,1,0:T(8,128)} %bitcast.3, s32[8]{0:T(128)} %pairing_ref.1), custom_call_target="tpu_custom_call" | custom-call | tf_op jit(solution)/shard_map/pallas_call | solution.py:1033
  6.9 64.5 %conditional.1 = ((f32[3584,128]{1,0:T(8,128)S(1)}, f32[1,8]{1,0:T(1,128)S(1)})) conditional(s32[]{:T(128)} %bitcast.1, (f32[2048,128]{1,0:T(8,128)S(1)}, f32[4,16,4096]{2,1,0:T(8,128)}, s32[16,32]{1,0:T(8,128)}, s32[8]{0:T(128)}) %tuple.59, (f32[2048,128]{1,0:T(8,128)S(1)}, f32[4,16,4096]{2,1,0:T(8,128)}, ...), branch_computations={%region_0.0_spmd, %region_1.0_spmd, %region_2.0_spmd, %region_3.0_... | conditional | bytes 8 | solution.py:1048
  7.2 64.1 %branch_16_fun.1 = (f32[3584,128]{1,0:T(8,128)S(1)}, f32[1,8]{1,0:T(1,128)S(1)}) custom-call(f32[2048,128]{1,0:T(8,128)S(1)} %get-tuple-element.200.first_ref, f32[4,16,4096]{2,1,0:T(8,128)} %get-tuple-element.201.analysis_ref, s32[16,32]{1,0:T(8,128)} %get-tuple-element.202.lab_ref, s32[8]{0:T(128)} %get-tuple-element.203.pairing_ref), custom_call_target="tpu_custom_call" | custom-call | tf_op jit(solution)/shard_map/cond/branch_16_fun/pallas_call | solution.py:1048
  71.4 3.3 %shard_map.60 = (f32[4,16,4096]{2,1,0:T(8,128)}, f32[1,8]{1,0:T(1,128)}) custom-call(f32[3584,128]{1,0:T(8,128)S(1)} %get-tuple-element.214.refs_0_, f32[1,8]{1,0:T(1,128)S(1)} %get-tuple-element.215.refs_1_), custom_call_target="tpu_custom_call" | custom-call | tf_op jit(solution)/shard_map/pallas_call | solution.py:1051
